TPU v7x, 256 devices: a whole 4x4x8 slice. The times are simulated.
256 devices in a mesh: peer: 8 (over x, z_hi), depth: 4 (over z_lo), row: 8 (over y, core).
Axes of the slice: x: 4, y: 4, z: 8 (z_hi: 2, z_lo: 4; z = z_hi * 4 + z_lo), core: 2. Of those that a mesh axis runs over, the one named last changes fastest.
Arguments:
- features: bfloat16 [12, 64, 2048], P('depth', 'row'), may hold values from -6 to 6
- labels: int32 [12, 64, 64], P('depth', 'row'), may hold values from 0 to 103
- conv_weights: bfloat16 [8, 4, 864, 32], P('peer'), may hold values from -0.21875 to 0.21875
- head_weights: bfloat16 [8, 32, 104], P('peer'), may hold values from -4 to 4
- matching: int32 [12, 8], P('depth'), may hold values from 0 to 7, each once within a row
Outputs:
- conv_grads: float32 [8, 4, 864, 32], P('peer')
- head_grads: float32 [8, 32, 104], P('peer')
- input_grads: bfloat16 [8, 12, 64, 2048], P('peer', 'depth', 'row')
Inputs may be any that keep to these rules, and one draw needn't show every extreme that they name: `matching`: in every depth plane every peer is distilled by exactly one peer.
All inputs are finite; a program needn't handle non-finite values.
Results may differ from a plain program's by a relative error of at most 0.019.
Values may be sent and summed in bfloat16 or wider, within the bound.
A program may use at most 64 MiB of HBM per device.

v0:
```python
import jax
import jax.numpy as jnp
from jax import lax
from jax.sharding import PartitionSpec as P


def with_halo(cells, sides, width):
    for axis, dim in sides:
        count = lax.axis_size(axis)
        ends = count - 1
        head = lax.slice_in_dim(cells, 0, width, axis=dim)
        tail = lax.slice_in_dim(cells, cells.shape[dim] - width, cells.shape[dim], axis=dim)
        cells = jnp.concatenate(
            [
                lax.ppermute(tail, axis, [(i, (i + 1) % count) for i in range(ends)]),
                cells,
                lax.ppermute(head, axis, [((i + 1) % count, i) for i in range(ends)]),
            ],
            axis=dim,
        )
    return cells


def columns(block, rows_out, width_out):
    pieces = []
    for depth_off in range(3):
        for row_off in range(3):
            for col_off in range(3):
                pieces.append(
                    block[depth_off, row_off : row_off + rows_out, col_off : col_off + width_out, :]
                )
    return jnp.concatenate(pieces, axis=-1).reshape(rows_out * width_out, -1)


def widened(padded, channels):
    depth_in, rows_in, merged = padded.shape
    volume = padded.reshape(depth_in, rows_in, merged // channels, channels)
    return jnp.pad(volume, ((0, 0), (0, 0), (1, 1), (0, 0)))


def convolve(padded, weight):
    channels = weight.shape[1]
    volume = widened(padded, channels)
    depth_out = padded.shape[0] - 2
    rows_out = padded.shape[1] - 2
    width_out = volume.shape[2] - 2

    def one_slice(depth_index):
        block = lax.dynamic_slice_in_dim(volume, depth_index, 3, 0)
        return jnp.dot(
            columns(block, rows_out, width_out), weight, preferred_element_type=jnp.float32
        )

    result = lax.map(one_slice, jnp.arange(depth_out, dtype=jnp.int32))
    return result.reshape(depth_out, rows_out, width_out * channels)


def weight_grad(padded, grad_out, channels):
    volume = widened(padded, channels)
    depth_out = padded.shape[0] - 2
    rows_out = padded.shape[1] - 2
    width_out = volume.shape[2] - 2
    grads = grad_out.reshape(depth_out, rows_out * width_out, channels)

    def accumulate(carry, depth_index):
        block = lax.dynamic_slice_in_dim(volume, depth_index, 3, 0)
        cols = columns(block, rows_out, width_out)
        slab = lax.dynamic_index_in_dim(grads, depth_index, 0, keepdims=False)
        contrib = lax.dot_general(
            cols, slab, (((0,), (0,)), ((), ())), preferred_element_type=jnp.float32
        )
        return (carry + contrib, None)

    init = jnp.zeros((27 * channels, channels), jnp.float32)
    result, unused = lax.scan(accumulate, init, jnp.arange(depth_out, dtype=jnp.int32))
    return result


def flipped(weight):
    channels = weight.shape[1]
    return (
        weight.reshape(27, channels, channels)[::-1]
        .transpose(0, 2, 1)
        .reshape(27 * channels, channels)
    )


def slope(pre):
    value = pre.astype(jnp.float32)
    sigma = jax.nn.sigmoid(value)
    return sigma * (1.0 + value * (1.0 - sigma))


def softmax_rows(hidden, head):
    logits = jnp.dot(hidden, head, preferred_element_type=jnp.float32)
    exponent = jnp.exp(logits)
    return exponent / jnp.sum(exponent, axis=1, keepdims=True)


def body(features, labels, conv_weights, head_weights, matching):
    channels = conv_weights.shape[3]
    classes = head_weights.shape[2]
    layers = conv_weights.shape[1]
    slab_depth, slab_rows, merged = features.shape
    width_cells = merged // channels
    voxels = slab_depth * slab_rows * width_cells
    padded_list = []
    pre_list = []
    current = features
    for layer in range(layers):
        padded = with_halo(current, (("depth", 0), ("row", 1)), 1)
        padded_list.append(padded)
        pre_full = convolve(padded, conv_weights[0, layer])
        pre_list.append(pre_full.astype(jnp.bfloat16))
        current = jax.nn.silu(pre_full).astype(jnp.bfloat16)
    hidden = current.reshape(voxels, channels)
    probs = softmax_rows(hidden, head_weights[0])
    own_peer = lax.axis_index("peer")
    partner = lax.dynamic_index_in_dim(matching, own_peer, 1, keepdims=False)
    own_probs = probs.astype(jnp.bfloat16).reshape(slab_depth, slab_rows, width_cells * classes)
    piece = lax.all_gather(own_probs[None], "peer", axis=0, tiled=True)
    owners = jnp.arange(piece.shape[0], dtype=jnp.int32)
    chosen = (owners[:, None] == partner[None, :]).astype(jnp.bfloat16)
    partner_probs = jnp.einsum("pd,pdrx->drx", chosen, piece, preferred_element_type=jnp.float32)
    partner_flat = partner_probs.reshape(voxels, classes)
    onehot = (labels.reshape(voxels, 1) == jnp.arange(classes, dtype=jnp.int32)[None, :]).astype(
        jnp.float32
    )
    mixed_grad = probs - 0.5 * onehot - 0.5 * partner_flat
    head_part = lax.dot_general(
        hidden,
        mixed_grad,
        (((0,), (0,)), ((), ())),
        precision=lax.Precision.HIGHEST,
        preferred_element_type=jnp.float32,
    )
    back_hidden = jnp.dot(
        mixed_grad, head_weights[0].astype(jnp.float32).T, precision=lax.Precision.HIGHEST
    )
    last_slope = slope(pre_list[layers - 1]).reshape(voxels, channels)
    grad_pre = (
        (back_hidden * last_slope).astype(jnp.bfloat16).reshape(slab_depth, slab_rows, merged)
    )
    kernel_grads = [None] * layers
    input_grad = None
    for layer in reversed(range(layers)):
        partial_grad = weight_grad(padded_list[layer], grad_pre, channels)
        kernel_grads[layer] = partial_grad
        padded_grad = with_halo(grad_pre, (("depth", 0), ("row", 1)), 1)
        back_input = convolve(padded_grad, flipped(conv_weights[0, layer]))
        if layer > 0:
            grad_pre = (back_input * slope(pre_list[layer - 1])).astype(jnp.bfloat16)
        else:
            input_grad = back_input.astype(jnp.bfloat16)
    stacked = jnp.stack(kernel_grads)
    head_total, stacked = (
        lax.psum(head_part.astype(jnp.bfloat16), ("depth", "row")).astype(jnp.float32),
        lax.psum(stacked.astype(jnp.bfloat16), ("depth", "row")).astype(jnp.float32),
    )
    return (stacked[None], head_total[None], input_grad[None])


def solution(mesh):
    placed = (
        P("depth", "row", None),
        P("depth", "row", None),
        P("peer", None, None, None),
        P("peer", None, None),
        P("depth", None),
    )
    return jax.shard_map(
        body,
        mesh=mesh,
        in_specs=placed,
        out_specs=(
            P("peer", None, None, None),
            P("peer", None, None),
            P("peer", "depth", "row", None),
        ),
        check_vma=False,
    )
```

profile of v0, /device:TPU:2, one launch (start us, length us, event | category | flops | bytes accessed | tf_op | source)
XLA Modules:
  0.0 996.8 jit_solution(811893436756225199)
XLA Ops:
  25.7 32.4 %while.124 = (s32[]{:T(128)}, f32[3,512,32]{1,2,0:T(8,128)}, s32[3]{0:T(128)S(1)}, bf16[5,10,66,32]{3,2,1,0:T(8,128)(2,1)S(1)}, bf16[864,32]{1,0:T(8,128)(2,1)},...) while((s32[]{:T(128)}, f32[3,512,32]{1,2,0:T(8,128)}, s32[3]{0:T(128)S(1)}, ...), condition=%wide.region_1.2_spmd, body=%wide.region_0.1_spmd.sunk | while | flops 28311560 | bytes 4710627 | solution.py:54
  30.2 4.3 concatenate.884
  41.0 4.3 concatenate.884
  51.8 4.3 concatenate.884
  65.4 4.2 collective-permute-done.5
  79.7 32.4 %while.125 = (s32[]{:T(128)}, f32[3,512,32]{1,2,0:T(8,128)}, s32[3]{0:T(128)S(1)}, bf16[5,10,66,32]{3,2,1,0:T(8,128)(2,1)S(1)}, bf16[864,32]{1,0:T(8,128)(2,1)},...) while((s32[]{:T(128)}, f32[3,512,32]{1,2,0:T(8,128)}, s32[3]{0:T(128)S(1)}, ...), condition=%wide.region_3.4_spmd, body=%wide.region_2.3_spmd.sunk | while | flops 28311560 | bytes 4710627 | solution.py:54
  84.2 4.3 concatenate.885
  95.0 4.3 concatenate.885
  105.8 4.3 concatenate.885
  119.0 4.2 collective-permute-done.9
  132.8 33.5 %while.126 = (s32[]{:T(128)}, f32[3,512,32]{1,2,0:T(8,128)}, s32[3]{0:T(128)}, bf16[5,10,66,32]{3,2,1,0:T(8,128)(2,1)S(1)}, bf16[864,32]{1,0:T(8,128)(2,1)}, /*index=5*/s32[]{:T(128)}, s32[]{:T(128)}, s32[]{:T(128)}, s32[]{}, s32[]{}) while((s32[]{:T(128)}, f32[3,512,32]{1,2,0:T(8,128)}, s32[3]{0:T(128)}, ...), condition=%wide.region_5.6_spmd, body=%wide.region_4.5_spmd.sunk | while | flops 28311560 | bytes 4710627 | solution.py:54
  137.9 4.1 concatenate.886
  149.1 4.1 concatenate.886
  171.7 4.2 collective-permute-done.13
  187.3 34.5 %while.127 = (s32[]{:T(128)}, f32[3,512,32]{1,2,0:T(8,128)}, s32[3]{0:T(128)S(1)}, bf16[5,10,66,32]{3,2,1,0:T(8,128)(2,1)S(1)}, bf16[864,32]{1,0:T(8,128)(2,1)},...) while((s32[]{:T(128)}, f32[3,512,32]{1,2,0:T(8,128)}, s32[3]{0:T(128)S(1)}, ...), condition=%wide.region_7.8_spmd, body=%wide.region_6.7_spmd.sunk | while | flops 28311560 | bytes 4743395 | solution.py:54
  191.9 4.6 concatenate.887
  203.4 4.6 concatenate.887
  214.9 4.6 concatenate.887
  241.1 72.2 %all-gather.2.cloned.1.call-done = bf16[8,3,8,6656]{3,2,1,0:T(8,128)(2,1)} async-done(((bf16[1,3,8,6656]{3,2,1,0:T(8,128)(2,1)}), bf16[8,3,8,6656]{3,2,1,0:T(8,128)(2,1)}) %all-gather.2.cloned.1.call-update) | async-done | bytes 2555920 | tf_op jit(solution)/shard_map/all_gather | solution.py:121
  330.1 5.1 collective-permute-start.16
  335.2 36.3 %while.135 = (s32[]{:T(128)}, f32[864,32]{0,1:T(8,128)S(1)}, s32[3]{0:T(128)S(1)}, bf16[5,10,66,32]{3,2,1,0:T(8,128)(2,1)S(1)}, bf16[3,512,32]{2,1,0:T(8,128)(2,...) while((s32[]{:T(128)}, f32[864,32]{0,1:T(8,128)S(1)}, ...), condition=%wide.region_22.23_spmd.clone, body=%wide.region_21.22_spmd.clone.sunk | while | flops 28366860 | bytes 4808974 | solution.py:75
  341.2 4.7 concatenate.895
  353.3 4.7 concatenate.895
  365.4 4.7 concatenate.895
  379.2 71.3 %psum.15 = bf16[1,32,104]{2,1,0:T(8,128)(2,1)S(1)} all-reduce(bf16[1,32,104]{2,1,0:T(8,128)(2,1)S(1)} %fusion.23), channel_id=1, replica_groups=mesh['peer'=8,'depth'=4,'row'=8] {'depth','row'}, use_global_device_ids=true, to_apply=%region_24.25 | all-reduce | flops 3328 | bytes 13312 | tf_op jit(solution)/shard_map/psum | solution.py:157
  454.9 34.6 %while.128 = (s32[]{:T(128)}, f32[3,512,32]{1,2,0:T(8,128)}, s32[3]{0:T(128)S(1)}, bf16[5,10,66,32]{3,2,1,0:T(8,128)(2,1)S(1)}, bf16[864,32]{1,0:T(8,128)(2,1)},...) while((s32[]{:T(128)}, f32[3,512,32]{1,2,0:T(8,128)}, s32[3]{0:T(128)S(1)}, ...), condition=%wide.region_10.11_spmd, body=%wide.region_9.10_spmd.sunk | while | flops 28311560 | bytes 4743395 | solution.py:54
  459.6 4.6 concatenate.888
  471.1 4.6 concatenate.888
  482.6 4.6 concatenate.888
  497.1 35.1 %while.134 = (s32[]{:T(128)}, f32[864,32]{0,1:T(8,128)}, s32[3]{0:T(128)S(1)}, bf16[5,10,66,32]{3,2,1,0:T(8,128)(2,1)S(1)}, bf16[3,512,32]{1,2,0:T(8,128)(2,1)},...) while((s32[]{:T(128)}, f32[864,32]{0,1:T(8,128)}, ...), condition=%wide.region_20.21_spmd.clone, body=%wide.region_19.20_spmd.clone.sunk | while | flops 28366860 | bytes 4681998 | solution.py:75
  540.4 31.8 %while.129 = (s32[]{:T(128)}, f32[3,512,32]{1,2,0:T(8,128)}, s32[3]{0:T(128)S(1)}, bf16[5,10,66,32]{3,2,1,0:T(8,128)(2,1)S(1)}, bf16[864,32]{1,0:T(8,128)(2,1)},...) while((s32[]{:T(128)}, f32[3,512,32]{1,2,0:T(8,128)}, s32[3]{0:T(128)S(1)}, ...), condition=%wide.region_12.13_spmd, body=%wide.region_11.12_spmd.sunk | while | flops 28311560 | bytes 4710627 | solution.py:54
  555.5 4.1 concatenate.889
  566.1 4.1 concatenate.889
  574.9 4.5 collective-permute-start.24
  589.6 35.8 %while.133 = (s32[]{:T(128)}, f32[864,32]{0,1:T(8,128)}, s32[3]{0:T(128)S(1)}, bf16[5,10,66,32]{3,2,1,0:T(8,128)(2,1)S(1)}, bf16[3,512,32]{1,2,0:T(8,128)(2,1)},...) while((s32[]{:T(128)}, f32[864,32]{0,1:T(8,128)}, ...), condition=%wide.region_18.19_spmd.clone, body=%wide.region_17.18_spmd.clone.sunk | while | flops 28366860 | bytes 4681998 | solution.py:75
  595.4 4.3 concatenate.893
  607.2 4.3 concatenate.893
  619.2 4.3 concatenate.893
  628.2 32.0 %while.130 = (s32[]{:T(128)}, f32[3,512,32]{1,2,0:T(8,128)}, s32[3]{0:T(128)S(1)}, bf16[5,10,66,32]{3,2,1,0:T(8,128)(2,1)S(1)}, bf16[864,32]{1,0:T(8,128)(2,1)},...) while((s32[]{:T(128)}, f32[3,512,32]{1,2,0:T(8,128)}, s32[3]{0:T(128)S(1)}, ...), condition=%wide.region_14.15_spmd, body=%wide.region_13.14_spmd.sunk | while | flops 28311560 | bytes 4710627 | solution.py:54
  664.0 35.8 %while.132 = (s32[]{:T(128)}, f32[864,32]{0,1:T(8,128)}, s32[3]{0:T(128)S(1)}, bf16[5,10,66,32]{3,2,1,0:T(8,128)(2,1)S(1)}, bf16[3,512,32]{1,2,0:T(8,128)(2,1)},...) while((s32[]{:T(128)}, f32[864,32]{0,1:T(8,128)}, ...), condition=%wide.region_16.17_spmd.clone, body=%wide.region_15.16_spmd.clone.sunk | while | flops 28366860 | bytes 4681998 | solution.py:75
  669.8 4.3 concatenate.892
  681.6 4.3 concatenate.892
  693.6 4.3 concatenate.892
  718.1 32.5 %while.131 = (s32[]{:T(128)}, bf16[3,512,32]{1,2,0:T(8,128)(2,1)}, s32[3]{0:T(128)S(1)}, bf16[5,10,66,32]{3,2,1,0:T(8,128)(2,1)S(1)}, bf16[864,32]{1,0:T(8,128)(...) while((s32[]{:T(128)}, bf16[3,512,32]{1,2,0:T(8,128)(2,1)}, s32[3]{0:T(128)S(1)}, ...), condition=%wide.region_26.27_spmd, body=%wide.region_25.26_spmd.sunk | while | flops 28311560 | bytes 4710627 | solution.py:54
  722.7 4.3 concatenate.891
  733.5 4.3 concatenate.891
  744.3 4.3 concatenate.891
  752.8 235.1 %all-reduce.10.cloned.1.call-done = bf16[1,4,864,32]{2,3,1,0:T(8,128)(2,1)} async-done(((bf16[1,4,864,32]{2,3,1,0:T(8,128)(2,1)}), bf16[1,4,864,32]{2,3,1,0:T(8,128)(2,1)}) %all-reduce.10.cloned.1.call-update) | async-done | bytes 221200 | tf_op jit(solution)/shard_map/psum | solution.py:158
  (373 shorter events, 371.6 us)
Async XLA Ops:
  7.2 215.7 %copy-start = (bf16[1,32,104]{2,1,0:T(8,128)(2,1)S(1)}, bf16[1,32,104]{2,1,0:T(8,128)(2,1)}, u32[]{:S(2)}) copy-start(bf16[1,32,104]{2,1,0:T(8,128)(2,1)} %param.32) | copy-start | bytes 19972
  7.2 306.2 %all-gather.2.cloned.1.call-start = ((), (), s32[]{:S(2)}) async-start(), calls=%async_computation | async-start | bytes 2875392 | tf_op jit(solution)/shard_map/all_gather | solution.py:121
  8.0 5.4 collective-permute-start
  11.8 5.8 collective-permute-start.1
  17.7 5.0 collective-permute-start.2
  19.0 4.9 collective-permute-start.3
  58.1 20.9 %copy-start.2 = (bf16[5,10,66,32]{3,2,1,0:T(8,128)(2,1)}, bf16[5,10,66,32]{3,2,1,0:T(8,128)(2,1)S(1)}, u32[]{:S(2)}) copy-start(bf16[5,10,66,32]{3,2,1,0:T(8,128)(2,1)S(1)} %get-tuple-element.2346) | copy-start | bytes 633604
  58.1 16.3 %copy-start.22 = (bf16[1,1,864,32]{2,3,1,0:T(8,128)(2,1)S(1)}, bf16[1,1,864,32]{2,3,1,0:T(8,128)(2,1)}, u32[]{:S(2)}) copy-start(bf16[1,1,864,32]{2,3,1,0:T(8,128)(2,1)} %get-tuple-element.912) | copy-start | bytes 165892
  59.9 18.0 %copy-start.11 = (f32[3,8,2048]{2,1,0:T(8,128)}, f32[3,8,2048]{2,1,0:T(8,128)S(1)}, u32[]{:S(2)}) copy-start(f32[3,8,2048]{2,1,0:T(8,128)S(1)} %reshape.761) | copy-start | bytes 589828
  60.0 5.4 collective-permute-start.4
  63.8 5.8 collective-permute-start.5
  69.7 5.5 collective-permute-start.6
  73.1 4.8 collective-permute-start.7
  112.1 16.2 %copy-start.21 = (bf16[1,1,864,32]{2,3,1,0:T(8,128)(2,1)S(1)}, bf16[1,1,864,32]{2,3,1,0:T(8,128)(2,1)}, u32[]{:S(2)}) copy-start(bf16[1,1,864,32]{2,3,1,0:T(8,128)(2,1)} %get-tuple-element.911) | copy-start | bytes 165892
  113.7 16.8 %copy-start.12 = (f32[3,8,2048]{2,1,0:T(8,128)}, f32[3,8,2048]{2,1,0:T(8,128)S(1)}, u32[]{:S(2)}) copy-start(f32[3,8,2048]{2,1,0:T(8,128)S(1)} %reshape.763) | copy-start | bytes 589828
  113.8 5.2 collective-permute-start.8
  117.4 5.8 collective-permute-start.9
  123.3 5.8 collective-permute-start.10
  126.5 4.0 collective-permute-start.11
  166.3 14.2 %copy-start.20 = (bf16[1,1,864,32]{2,3,1,0:T(8,128)(2,1)S(1)}, bf16[1,1,864,32]{2,3,1,0:T(8,128)(2,1)}, u32[]{:S(2)}) copy-start(bf16[1,1,864,32]{2,3,1,0:T(8,128)(2,1)} %get-tuple-element.910) | copy-start | bytes 165892
  167.9 15.8 %copy-start.13 = (f32[3,8,2048]{2,1,0:T(8,128)}, f32[3,8,2048]{2,1,0:T(8,128)S(1)}, u32[]{:S(2)}) copy-start(f32[3,8,2048]{2,1,0:T(8,128)S(1)} %reshape.765) | copy-start | bytes 589828
  168.0 3.8 collective-permute-start.12
  170.2 5.8 collective-permute-start.13
  176.0 5.3 collective-permute-start.14
  179.2 4.2 collective-permute-start.15
  221.8 12.9 %copy-start.5 = (bf16[864,32]{1,0:T(8,128)(2,1)S(1)}, bf16[864,32]{1,0:T(8,128)(2,1)}, u32[]{:S(2)}) copy-start(bf16[864,32]{1,0:T(8,128)(2,1)} %get-tuple-element.2351) | copy-start | bytes 165892
  222.8 14.3 %copy-start.6 = (bf16[864,32]{1,0:T(8,128)(2,1)S(1)}, bf16[864,32]{1,0:T(8,128)(2,1)}, u32[]{:S(2)}) copy-start(bf16[864,32]{1,0:T(8,128)(2,1)} %get-tuple-element.2352) | copy-start | bytes 165892
  229.0 758.9 %all-reduce.10.cloned.1.call-start = ((), (), s32[]{:S(2)}) async-start(), calls=%async_computation.1 | async-start | bytes 458752 | tf_op jit(solution)/shard_map/psum | solution.py:158
  327.9 45.9 %collective-permute-start.17 = (bf16[1,8,2048]{2,1,0:T(8,128)(2,1)}, bf16[1,8,2048]{2,1,0:T(8,128)(2,1)}, u32[]{:S(2)}, u32[]{:S(2)}) collective-permute-start(bf16[1,8,2048]{2,1,0:T(8,128)(2,1)} %slice.1113), channel_id=1, source_target_pairs={{8,0},{16,8},{24,16},{9,1},{17,9},{25,17},{10,2},{18,10},{26,18},{... | collective-permute-start | bytes 98312 | tf_op jit(solution)/shard_map/ppermute | solution.py:17
  330.1 42.9 %collective-permute-start.16 = (bf16[1,8,2048]{2,1,0:T(8,128)(2,1)}, bf16[1,8,2048]{2,1,0:T(8,128)(2,1)}, u32[]{:S(2)}, u32[]{:S(2)}) collective-permute-start(bf16[1,8,2048]{2,1,0:T(8,128)(2,1)} %slice.1111), channel_id=1, source_target_pairs={{0,8},{8,16},{16,24},{1,9},{9,17},{17,25},{2,10},{10,18},{18,26},{... | collective-permute-start | bytes 98312 | tf_op jit(solution)/shard_map/ppermute | solution.py:15
  335.2 42.0 %copy-start.28 = (s32[1536]{0:T(1024)S(1)}, s32[1536]{0:T(1024)}, u32[]{:S(2)}) copy-start(s32[1536]{0:T(1024)} %eq.30) | copy-start | bytes 18436
  371.6 79.7 %copy-start.7 = (f32[864,32]{0,1:T(8,128)}, f32[864,32]{0,1:T(8,128)S(1)}, u32[]{:S(2)}) copy-start(f32[864,32]{0,1:T(8,128)S(1)} %get-tuple-element.337) | copy-start | bytes 331780
  374.7 76.4 %collective-permute-start.18 = (bf16[5,1,2048]{2,1,0:T(2,128)(2,1)S(1)}, bf16[5,1,2048]{2,1,0:T(2,128)(2,1)S(1)}, u32[]{:S(2)}, u32[]{:S(2)}) collective-permute-start(bf16[5,1,2048]{2,1,0:T(2,128)(2,1)S(1)} %get-tuple-element.920), channel_id=1, source_target_pairs={{0,1},{1,2},{2,3},{3,4},{4,5},{5,6},{6,7},{8,9},{9,10},{10,11},{11... | collective-permute-start | bytes 61448 | tf_op jit(solution)/shard_map/ppermute | solution.py:15
  376.0 75.1 %collective-permute-start.19 = (bf16[5,1,2048]{2,1,0:T(2,128)(2,1)S(1)}, bf16[5,1,2048]{2,1,0:T(2,128)(2,1)S(1)}, u32[]{:S(2)}, u32[]{:S(2)}) collective-permute-start(bf16[5,1,2048]{2,1,0:T(2,128)(2,1)S(1)} %get-tuple-element.921), channel_id=1, source_target_pairs={{1,0},{2,1},{3,2},{4,3},{5,4},{6,5},{7,6},{9,8},{10,9},{11,10},{12... | collective-permute-start | bytes 61448 | tf_op jit(solution)/shard_map/ppermute | solution.py:17
  493.7 38.5 %collective-permute-start.20 = (bf16[1,8,2048]{2,1,0:T(8,128)(2,1)}, bf16[1,8,2048]{2,1,0:T(8,128)(2,1)}, u32[]{:S(2)}, u32[]{:S(2)}) collective-permute-start(bf16[1,8,2048]{2,1,0:T(8,128)(2,1)} %get-tuple-element.934), channel_id=1, source_target_pairs={{0,8},{8,16},{16,24},{1,9},{9,17},{17,25},{2,10},{10,18},{18,26},{... | collective-permute-start | bytes 98312 | tf_op jit(solution)/shard_map/ppermute | solution.py:15
  495.6 36.7 %collective-permute-start.21 = (bf16[1,8,2048]{2,1,0:T(8,128)(2,1)}, bf16[1,8,2048]{2,1,0:T(8,128)(2,1)}, u32[]{:S(2)}, u32[]{:S(2)}) collective-permute-start(bf16[1,8,2048]{2,1,0:T(8,128)(2,1)} %get-tuple-element.935), channel_id=1, source_target_pairs={{8,0},{16,8},{24,16},{9,1},{17,9},{25,17},{10,2},{18,10},{26,18},{... | collective-permute-start | bytes 98312 | tf_op jit(solution)/shard_map/ppermute | solution.py:17
  533.3 4.2 collective-permute-start.22
  534.6 3.1 collective-permute-start.23
  574.9 6.6 collective-permute-start.24
  579.4 5.8 collective-permute-start.25
  586.0 39.4 %collective-permute-start.26 = (bf16[5,1,2048]{2,1,0:T(2,128)(2,1)}, bf16[5,1,2048]{2,1,0:T(2,128)(2,1)}, u32[]{:S(2)}, u32[]{:S(2)}) collective-permute-start(bf16[5,1,2048]{2,1,0:T(2,128)(2,1)} %get-tuple-element.916), channel_id=1, source_target_pairs={{0,1},{1,2},{2,3},{3,4},{4,5},{5,6},{6,7},{8,9},{9,10},{10,11},{11... | collective-permute-start | bytes 61448 | tf_op jit(solution)/shard_map/ppermute | solution.py:15
  588.3 37.1 %collective-permute-start.27 = (bf16[5,1,2048]{2,1,0:T(2,128)(2,1)}, bf16[5,1,2048]{2,1,0:T(2,128)(2,1)}, u32[]{:S(2)}, u32[]{:S(2)}) collective-permute-start(bf16[5,1,2048]{2,1,0:T(2,128)(2,1)} %get-tuple-element.917), channel_id=1, source_target_pairs={{1,0},{2,1},{3,2},{4,3},{5,4},{6,5},{7,6},{9,8},{10,9},{11,10},{12... | collective-permute-start | bytes 61448 | tf_op jit(solution)/shard_map/ppermute | solution.py:17
  628.2 35.8 %copy-start.3 = (bf16[5,10,66,32]{3,2,1,0:T(8,128)(2,1)S(1)}, bf16[5,10,66,32]{3,2,1,0:T(8,128)(2,1)}, u32[]{:S(2)}) copy-start(bf16[5,10,66,32]{3,2,1,0:T(8,128)(2,1)} %copy-done.2) | copy-start | bytes 633604
  702.3 4.8 collective-permute-start.28
  704.8 6.0 collective-permute-start.29
  710.9 4.8 collective-permute-start.30
  712.8 4.2 collective-permute-start.31
  750.6 239.0 %copy-start.1 = (bf16[1,32,104]{2,1,0:T(8,128)(2,1)S(1)}, bf16[1,32,104]{2,1,0:T(8,128)(2,1)}, u32[]{:S(2)}) copy-start(bf16[1,32,104]{2,1,0:T(8,128)(2,1)} %param.32) | copy-start | bytes 19972
  (16 other events, 85.2 us)
Sparse Core Ops, SparseCore 0:
  229.1 84.2 all-gather.1
  715.9 271.9 all-reduce.9
where the time goes:
time: 1020 us; the launch traced here: 997 us
  waiting for transfers between devices  341 us (33%)
  local copies, waits for them, and re-layouts  318 us (31%)
  loops' own time  85.7 us (8%)
  matrix products  76.3 us (7%)
  blocking collectives  71.3 us (7%)
  starting transfers between devices  66.9 us (7%)
  other arithmetic  22 us (2%)
  between operations  15.4 us (2%)
    psum x1, waiting for transfers between devices, body(): lax.psum(stacked.astype(jnp.bfloat16), ('depth', 'row')).astype(jnp.float32)  235 us
    concatenate x36, local copies, waits for them, and re-layouts, columns(): return jnp.concatenate(pieces, axis=-1).reshape(rows_out * width_out, -1)  156 us
    slice x36, local copies, waits for them, and re-layouts, columns(): block[depth_off, row_off:row_off + rows_out, col_off:col_off + width_out, :]  73.3 us
    all_gather x1, waiting for transfers between devices, body(): piece = lax.all_gather(own_probs[None], 'peer', axis=0, tiled=True)  72.2 us
    psum x1, blocking collectives, body(): lax.psum(head_part.astype(jnp.bfloat16), ('depth', 'row'))  71.3 us
    dot_general x24, matrix products, one_slice(): jnp.dot(columns(block, rows_out, width_out), weight, preferred_element_ty...  48.5 us
    another operation x8, loops' own time, convolve(): result = lax.map(one_slice, jnp.arange(depth_out, dtype=jnp.int32))  46.9 us
    ppermute x16, starting transfers between devices, with_halo(): lax.ppermute(tail, axis, [(i, (i + 1) % count) for i in range(ends)])  45.3 us
  transfers between devices with their start and end apart: 34, of which 18 were waited for; matrix products, arithmetic and copies ran while one was open for 14% of the time, Pallas kernels for 0%

commit v1 on v0

--- a/solution.py
+++ b/solution.py
@@ -154,7 +154,7 @@
             input_grad = back_input.astype(jnp.bfloat16)
     stacked = jnp.stack(kernel_grads)
     head_total, stacked = (
-        lax.psum(head_part.astype(jnp.bfloat16), ("depth", "row")).astype(jnp.float32),
+        lax.psum(lax.psum(head_part.astype(jnp.bfloat16), "depth"), "row").astype(jnp.float32),
         lax.psum(stacked.astype(jnp.bfloat16), ("depth", "row")).astype(jnp.float32),
     )
     return (stacked[None], head_total[None], input_grad[None])

time: 1020 us -> 974 us (0.955)
  blocking collectives: 71.3 us -> 23.6 us
    psum x1 -> x2, blocking collectives: 71.3 us -> 23.6 us  [the longest x1 15.1 us: body(): lax.psum(lax.psum(head_part.astype(jnp.bfloat16), 'depth'), 'row')]
where the time goes in v1:
time: 974 us; the launch traced here: 955 us
  waiting for transfers between devices  342 us (35%)
  local copies, waits for them, and re-layouts  319 us (33%)
  loops' own time  86.3 us (9%)
  matrix products  76.3 us (8%)
  starting transfers between devices  70.7 us (7%)
  blocking collectives  23.6 us (2%)
  other arithmetic  22.1 us (2%)
  between operations  15.4 us (2%)
    psum x1, waiting for transfers between devices, body(): lax.psum(stacked.astype(jnp.bfloat16), ('depth', 'row')).astype(jnp.float32)  235 us
    concatenate x36, local copies, waits for them, and re-layouts, columns(): return jnp.concatenate(pieces, axis=-1).reshape(rows_out * width_out, -1)  156 us
    slice x36, local copies, waits for them, and re-layouts, columns(): block[depth_off, row_off:row_off + rows_out, col_off:col_off + width_out, :]  73.4 us
    all_gather x1, waiting for transfers between devices, body(): piece = lax.all_gather(own_probs[None], 'peer', axis=0, tiled=True)  72.3 us
    ppermute x16, starting transfers between devices, with_halo(): lax.ppermute(tail, axis, [(i, (i + 1) % count) for i in range(ends)])  49.1 us
    dot_general x24, matrix products, one_slice(): jnp.dot(columns(block, rows_out, width_out), weight, preferred_element_ty...  48.4 us
    another operation x8, loops' own time, convolve(): result = lax.map(one_slice, jnp.arange(depth_out, dtype=jnp.int32))  46.9 us
    another operation x4, loops' own time, weight_grad(): lax.scan(accumulate, init, jnp.arange(depth_out, dtype=jnp.int32))  39.4 us
  transfers between devices with their start and end apart: 34, of which 18 were waited for; matrix products, arithmetic and copies ran while one was open for 14% of the time, Pallas kernels for 0%

profile of v1, /device:TPU:2, one launch (start us, length us, event | category | flops | bytes accessed | tf_op | source)
XLA Modules:
  0.0 955.0 jit_solution(17293260210754162338)
XLA Ops:
  25.7 32.3 %while.124 = (s32[]{:T(128)}, f32[3,512,32]{1,2,0:T(8,128)}, s32[3]{0:T(128)S(1)}, bf16[5,10,66,32]{3,2,1,0:T(8,128)(2,1)S(1)}, bf16[864,32]{1,0:T(8,128)(2,1)},...) while((s32[]{:T(128)}, f32[3,512,32]{1,2,0:T(8,128)}, s32[3]{0:T(128)S(1)}, ...), condition=%wide.region_1.2_spmd, body=%wide.region_0.1_spmd.sunk | while | flops 28311560 | bytes 4710627 | solution.py:54
  30.2 4.3 concatenate.884
  40.9 4.3 concatenate.884
  51.7 4.3 concatenate.884
  65.3 4.2 collective-permute-done.5
  79.6 32.4 %while.125 = (s32[]{:T(128)}, f32[3,512,32]{1,2,0:T(8,128)}, s32[3]{0:T(128)S(1)}, bf16[5,10,66,32]{3,2,1,0:T(8,128)(2,1)S(1)}, bf16[864,32]{1,0:T(8,128)(2,1)},...) while((s32[]{:T(128)}, f32[3,512,32]{1,2,0:T(8,128)}, s32[3]{0:T(128)S(1)}, ...), condition=%wide.region_3.4_spmd, body=%wide.region_2.3_spmd.sunk | while | flops 28311560 | bytes 4710627 | solution.py:54
  84.1 4.3 concatenate.885
  94.9 4.3 concatenate.885
  105.7 4.3 concatenate.885
  118.9 4.2 collective-permute-done.9
  132.7 33.6 %while.126 = (s32[]{:T(128)}, f32[3,512,32]{1,2,0:T(8,128)}, s32[3]{0:T(128)}, bf16[5,10,66,32]{3,2,1,0:T(8,128)(2,1)S(1)}, bf16[864,32]{1,0:T(8,128)(2,1)}, /*index=5*/s32[]{:T(128)}, s32[]{:T(128)}, s32[]{:T(128)}, s32[]{}, s32[]{}) while((s32[]{:T(128)}, f32[3,512,32]{1,2,0:T(8,128)}, s32[3]{0:T(128)}, ...), condition=%wide.region_5.6_spmd, body=%wide.region_4.5_spmd.sunk | while | flops 28311560 | bytes 4710627 | solution.py:54
  171.8 4.2 collective-permute-done.13
  187.4 34.5 %while.127 = (s32[]{:T(128)}, f32[3,512,32]{1,2,0:T(8,128)}, s32[3]{0:T(128)S(1)}, bf16[5,10,66,32]{3,2,1,0:T(8,128)(2,1)S(1)}, bf16[864,32]{1,0:T(8,128)(2,1)},...) while((s32[]{:T(128)}, f32[3,512,32]{1,2,0:T(8,128)}, s32[3]{0:T(128)S(1)}, ...), condition=%wide.region_7.8_spmd, body=%wide.region_6.7_spmd.sunk | while | flops 28311560 | bytes 4743395 | solution.py:54
  192.0 4.7 concatenate.887
  203.5 4.7 concatenate.887
  215.0 4.7 concatenate.887
  241.3 72.3 %all-gather.2.cloned.1.call-done = bf16[8,3,8,6656]{3,2,1,0:T(8,128)(2,1)} async-done(((bf16[1,3,8,6656]{3,2,1,0:T(8,128)(2,1)}), bf16[8,3,8,6656]{3,2,1,0:T(8,128)(2,1)}) %all-gather.2.cloned.1.call-update) | async-done | bytes 2555920 | tf_op jit(solution)/shard_map/all_gather | solution.py:121
  330.2 5.2 collective-permute-start.16
  335.4 37.1 %while.135 = (s32[]{:T(128)}, f32[864,32]{0,1:T(8,128)S(1)}, s32[3]{0:T(128)S(1)}, bf16[5,10,66,32]{3,2,1,0:T(8,128)(2,1)S(1)}, bf16[3,512,32]{2,1,0:T(8,128)(2,...) while((s32[]{:T(128)}, f32[864,32]{0,1:T(8,128)S(1)}, ...), condition=%wide.region_22.23_spmd.clone, body=%wide.region_21.22_spmd.clone.sunk | while | flops 28366860 | bytes 4808974 | solution.py:75
  341.6 4.7 concatenate.895
  354.0 4.7 concatenate.895
  366.4 4.7 concatenate.895
  380.2 8.5 psum.22
  388.7 15.1 %psum.23 = bf16[1,32,104]{2,1,0:T(8,128)(2,1)S(1)} all-reduce(bf16[1,32,104]{2,1,0:T(8,128)(2,1)S(1)} %bitcast.1531), channel_id=1, replica_groups=mesh['peer'=8,'depth'=4,'row'=8] {'row'}, use_global_device_ids=true, to_apply=%region_25.26 | all-reduce | flops 3328 | bytes 13312 | tf_op jit(solution)/shard_map/psum | solution.py:157
  408.2 34.6 %while.128 = (s32[]{:T(128)}, f32[3,512,32]{1,2,0:T(8,128)}, s32[3]{0:T(128)S(1)}, bf16[5,10,66,32]{3,2,1,0:T(8,128)(2,1)S(1)}, bf16[864,32]{1,0:T(8,128)(2,1)},...) while((s32[]{:T(128)}, f32[3,512,32]{1,2,0:T(8,128)}, s32[3]{0:T(128)S(1)}, ...), condition=%wide.region_10.11_spmd, body=%wide.region_9.10_spmd.sunk | while | flops 28311560 | bytes 4743395 | solution.py:54
  412.8 4.7 concatenate.888
  424.4 4.7 concatenate.888
  435.9 4.7 concatenate.888
  446.9 4.4 collective-permute-start.20
  452.9 35.3 %while.134 = (s32[]{:T(128)}, f32[864,32]{0,1:T(8,128)}, s32[3]{0:T(128)S(1)}, bf16[5,10,66,32]{3,2,1,0:T(8,128)(2,1)S(1)}, bf16[3,512,32]{1,2,0:T(8,128)(2,1)},...) while((s32[]{:T(128)}, f32[864,32]{0,1:T(8,128)}, ...), condition=%wide.region_20.21_spmd.clone, body=%wide.region_19.20_spmd.clone.sunk | while | flops 28366860 | bytes 4681998 | solution.py:75
  458.7 4.1 concatenate.894
  470.4 4.1 concatenate.894
  497.0 31.8 %while.129 = (s32[]{:T(128)}, f32[3,512,32]{1,2,0:T(8,128)}, s32[3]{0:T(128)S(1)}, bf16[5,10,66,32]{3,2,1,0:T(8,128)(2,1)S(1)}, bf16[864,32]{1,0:T(8,128)(2,1)},...) while((s32[]{:T(128)}, f32[3,512,32]{1,2,0:T(8,128)}, s32[3]{0:T(128)S(1)}, ...), condition=%wide.region_12.13_spmd, body=%wide.region_11.12_spmd.sunk | while | flops 28311560 | bytes 4710627 | solution.py:54
  531.5 4.3 collective-permute-start.24
  546.9 35.8 %while.133 = (s32[]{:T(128)}, f32[864,32]{0,1:T(8,128)}, s32[3]{0:T(128)S(1)}, bf16[5,10,66,32]{3,2,1,0:T(8,128)(2,1)S(1)}, bf16[3,512,32]{1,2,0:T(8,128)(2,1)},...) while((s32[]{:T(128)}, f32[864,32]{0,1:T(8,128)}, ...), condition=%wide.region_18.19_spmd.clone, body=%wide.region_17.18_spmd.clone.sunk | while | flops 28366860 | bytes 4681998 | solution.py:75
  552.8 4.3 concatenate.893
  564.6 4.3 concatenate.893
  576.6 4.3 concatenate.893
  585.5 31.9 %while.130 = (s32[]{:T(128)}, f32[3,512,32]{1,2,0:T(8,128)}, s32[3]{0:T(128)S(1)}, bf16[5,10,66,32]{3,2,1,0:T(8,128)(2,1)S(1)}, bf16[864,32]{1,0:T(8,128)(2,1)},...) while((s32[]{:T(128)}, f32[3,512,32]{1,2,0:T(8,128)}, s32[3]{0:T(128)S(1)}, ...), condition=%wide.region_14.15_spmd, body=%wide.region_13.14_spmd.sunk | while | flops 28311560 | bytes 4710627 | solution.py:54
  621.3 35.8 %while.132 = (s32[]{:T(128)}, f32[864,32]{0,1:T(8,128)}, s32[3]{0:T(128)S(1)}, bf16[5,10,66,32]{3,2,1,0:T(8,128)(2,1)S(1)}, bf16[3,512,32]{1,2,0:T(8,128)(2,1)},...) while((s32[]{:T(128)}, f32[864,32]{0,1:T(8,128)}, ...), condition=%wide.region_16.17_spmd.clone, body=%wide.region_15.16_spmd.clone.sunk | while | flops 28366860 | bytes 4681998 | solution.py:75
  627.1 4.3 concatenate.892
  638.9 4.3 concatenate.892
  650.9 4.3 concatenate.892
  676.2 32.5 %while.131 = (s32[]{:T(128)}, bf16[3,512,32]{1,2,0:T(8,128)(2,1)}, s32[3]{0:T(128)S(1)}, bf16[5,10,66,32]{3,2,1,0:T(8,128)(2,1)S(1)}, bf16[864,32]{1,0:T(8,128)(...) while((s32[]{:T(128)}, bf16[3,512,32]{1,2,0:T(8,128)(2,1)}, s32[3]{0:T(128)S(1)}, ...), condition=%wide.region_27.28_spmd, body=%wide.region_26.27_spmd.sunk | while | flops 28311560 | bytes 4710627 | solution.py:54
  680.8 4.3 concatenate.891
  691.6 4.3 concatenate.891
  702.5 4.3 concatenate.891
  710.9 235.1 %all-reduce.10.cloned.1.call-done = bf16[1,4,864,32]{2,3,1,0:T(8,128)(2,1)} async-done(((bf16[1,4,864,32]{2,3,1,0:T(8,128)(2,1)}), bf16[1,4,864,32]{2,3,1,0:T(8,128)(2,1)}) %all-reduce.10.cloned.1.call-update) | async-done | bytes 221200 | tf_op jit(solution)/shard_map/psum | solution.py:158
  (374 shorter events, 380.8 us)
Async XLA Ops:
  7.2 215.8 %copy-start = (bf16[1,32,104]{2,1,0:T(8,128)(2,1)S(1)}, bf16[1,32,104]{2,1,0:T(8,128)(2,1)}, u32[]{:S(2)}) copy-start(bf16[1,32,104]{2,1,0:T(8,128)(2,1)} %param.32) | copy-start | bytes 19972
  7.2 306.3 %all-gather.2.cloned.1.call-start = ((), (), s32[]{:S(2)}) async-start(), calls=%async_computation | async-start | bytes 2875392 | tf_op jit(solution)/shard_map/all_gather | solution.py:121
  8.0 5.4 collective-permute-start
  11.8 5.8 collective-permute-start.1
  17.7 5.0 collective-permute-start.2
  19.0 4.9 collective-permute-start.3
  58.0 20.9 %copy-start.2 = (bf16[5,10,66,32]{3,2,1,0:T(8,128)(2,1)}, bf16[5,10,66,32]{3,2,1,0:T(8,128)(2,1)S(1)}, u32[]{:S(2)}) copy-start(bf16[5,10,66,32]{3,2,1,0:T(8,128)(2,1)S(1)} %get-tuple-element.2346) | copy-start | bytes 633604
  58.0 16.3 %copy-start.22 = (bf16[1,1,864,32]{2,3,1,0:T(8,128)(2,1)S(1)}, bf16[1,1,864,32]{2,3,1,0:T(8,128)(2,1)}, u32[]{:S(2)}) copy-start(bf16[1,1,864,32]{2,3,1,0:T(8,128)(2,1)} %get-tuple-element.912) | copy-start | bytes 165892
  59.8 18.0 %copy-start.11 = (f32[3,8,2048]{2,1,0:T(8,128)}, f32[3,8,2048]{2,1,0:T(8,128)S(1)}, u32[]{:S(2)}) copy-start(f32[3,8,2048]{2,1,0:T(8,128)S(1)} %reshape.761) | copy-start | bytes 589828
  59.9 5.4 collective-permute-start.4
  63.7 5.8 collective-permute-start.5
  69.6 5.5 collective-permute-start.6
  73.0 4.8 collective-permute-start.7
  112.0 16.1 %copy-start.21 = (bf16[1,1,864,32]{2,3,1,0:T(8,128)(2,1)S(1)}, bf16[1,1,864,32]{2,3,1,0:T(8,128)(2,1)}, u32[]{:S(2)}) copy-start(bf16[1,1,864,32]{2,3,1,0:T(8,128)(2,1)} %get-tuple-element.911) | copy-start | bytes 165892
  113.6 16.8 %copy-start.12 = (f32[3,8,2048]{2,1,0:T(8,128)}, f32[3,8,2048]{2,1,0:T(8,128)S(1)}, u32[]{:S(2)}) copy-start(f32[3,8,2048]{2,1,0:T(8,128)S(1)} %reshape.763) | copy-start | bytes 589828
  113.7 5.2 collective-permute-start.8
  117.3 5.8 collective-permute-start.9
  123.2 5.8 collective-permute-start.10
  126.4 4.0 collective-permute-start.11
  166.4 14.2 %copy-start.20 = (bf16[1,1,864,32]{2,3,1,0:T(8,128)(2,1)S(1)}, bf16[1,1,864,32]{2,3,1,0:T(8,128)(2,1)}, u32[]{:S(2)}) copy-start(bf16[1,1,864,32]{2,3,1,0:T(8,128)(2,1)} %get-tuple-element.910) | copy-start | bytes 165892
  167.9 15.8 %copy-start.13 = (f32[3,8,2048]{2,1,0:T(8,128)}, f32[3,8,2048]{2,1,0:T(8,128)S(1)}, u32[]{:S(2)}) copy-start(f32[3,8,2048]{2,1,0:T(8,128)S(1)} %reshape.765) | copy-start | bytes 589828
  168.0 3.8 collective-permute-start.12
  170.2 5.8 collective-permute-start.13
  176.1 5.3 collective-permute-start.14
  179.3 4.2 collective-permute-start.15
  221.9 12.9 %copy-start.5 = (bf16[864,32]{1,0:T(8,128)(2,1)S(1)}, bf16[864,32]{1,0:T(8,128)(2,1)}, u32[]{:S(2)}) copy-start(bf16[864,32]{1,0:T(8,128)(2,1)} %get-tuple-element.2351) | copy-start | bytes 165892
  223.0 14.3 %copy-start.6 = (bf16[864,32]{1,0:T(8,128)(2,1)S(1)}, bf16[864,32]{1,0:T(8,128)(2,1)}, u32[]{:S(2)}) copy-start(bf16[864,32]{1,0:T(8,128)(2,1)} %get-tuple-element.2352) | copy-start | bytes 165892
  229.1 716.9 %all-reduce.10.cloned.1.call-start = ((), (), s32[]{:S(2)}) async-start(), calls=%async_computation.1 | async-start | bytes 458752 | tf_op jit(solution)/shard_map/psum | solution.py:158
  328.0 46.8 %collective-permute-start.17 = (bf16[1,8,2048]{2,1,0:T(8,128)(2,1)}, bf16[1,8,2048]{2,1,0:T(8,128)(2,1)}, u32[]{:S(2)}, u32[]{:S(2)}) collective-permute-start(bf16[1,8,2048]{2,1,0:T(8,128)(2,1)} %slice.1113), channel_id=1, source_target_pairs={{8,0},{16,8},{24,16},{9,1},{17,9},{25,17},{10,2},{18,10},{26,18},{... | collective-permute-start | bytes 98312 | tf_op jit(solution)/shard_map/ppermute | solution.py:17
  330.2 43.8 %collective-permute-start.16 = (bf16[1,8,2048]{2,1,0:T(8,128)(2,1)}, bf16[1,8,2048]{2,1,0:T(8,128)(2,1)}, u32[]{:S(2)}, u32[]{:S(2)}) collective-permute-start(bf16[1,8,2048]{2,1,0:T(8,128)(2,1)} %slice.1111), channel_id=1, source_target_pairs={{0,8},{8,16},{16,24},{1,9},{9,17},{17,25},{2,10},{10,18},{18,26},{... | collective-permute-start | bytes 98312 | tf_op jit(solution)/shard_map/ppermute | solution.py:15
  335.4 42.9 %copy-start.28 = (s32[1536]{0:T(1024)S(1)}, s32[1536]{0:T(1024)}, u32[]{:S(2)}) copy-start(s32[1536]{0:T(1024)} %eq.30) | copy-start | bytes 18436
  372.5 32.0 %copy-start.7 = (f32[864,32]{0,1:T(8,128)}, f32[864,32]{0,1:T(8,128)S(1)}, u32[]{:S(2)}) copy-start(f32[864,32]{0,1:T(8,128)S(1)} %get-tuple-element.337) | copy-start | bytes 331780
  375.6 28.7 %collective-permute-start.18 = (bf16[5,1,2048]{2,1,0:T(2,128)(2,1)S(1)}, bf16[5,1,2048]{2,1,0:T(2,128)(2,1)S(1)}, u32[]{:S(2)}, u32[]{:S(2)}) collective-permute-start(bf16[5,1,2048]{2,1,0:T(2,128)(2,1)S(1)} %get-tuple-element.920), channel_id=1, source_target_pairs={{0,1},{1,2},{2,3},{3,4},{4,5},{5,6},{6,7},{8,9},{9,10},{10,11},{11... | collective-permute-start | bytes 61448 | tf_op jit(solution)/shard_map/ppermute | solution.py:15
  376.9 27.4 %collective-permute-start.19 = (bf16[5,1,2048]{2,1,0:T(2,128)(2,1)S(1)}, bf16[5,1,2048]{2,1,0:T(2,128)(2,1)S(1)}, u32[]{:S(2)}, u32[]{:S(2)}) collective-permute-start(bf16[5,1,2048]{2,1,0:T(2,128)(2,1)S(1)} %get-tuple-element.921), channel_id=1, source_target_pairs={{1,0},{2,1},{3,2},{4,3},{5,4},{6,5},{7,6},{9,8},{10,9},{11,10},{12... | collective-permute-start | bytes 61448 | tf_op jit(solution)/shard_map/ppermute | solution.py:17
  446.9 41.2 %collective-permute-start.20 = (bf16[1,8,2048]{2,1,0:T(8,128)(2,1)}, bf16[1,8,2048]{2,1,0:T(8,128)(2,1)}, u32[]{:S(2)}, u32[]{:S(2)}) collective-permute-start(bf16[1,8,2048]{2,1,0:T(8,128)(2,1)} %get-tuple-element.934), channel_id=1, source_target_pairs={{0,8},{8,16},{16,24},{1,9},{9,17},{17,25},{2,10},{10,18},{18,26},{... | collective-permute-start | bytes 98312 | tf_op jit(solution)/shard_map/ppermute | solution.py:15
  451.4 36.8 %collective-permute-start.21 = (bf16[1,8,2048]{2,1,0:T(8,128)(2,1)}, bf16[1,8,2048]{2,1,0:T(8,128)(2,1)}, u32[]{:S(2)}, u32[]{:S(2)}) collective-permute-start(bf16[1,8,2048]{2,1,0:T(8,128)(2,1)} %get-tuple-element.935), channel_id=1, source_target_pairs={{8,0},{16,8},{24,16},{9,1},{17,9},{25,17},{10,2},{18,10},{26,18},{... | collective-permute-start | bytes 98312 | tf_op jit(solution)/shard_map/ppermute | solution.py:17
  489.2 4.9 collective-permute-start.22
  491.2 3.1 collective-permute-start.23
  531.5 6.3 collective-permute-start.24
  535.8 5.8 collective-permute-start.25
  542.3 40.5 %collective-permute-start.26 = (bf16[5,1,2048]{2,1,0:T(2,128)(2,1)}, bf16[5,1,2048]{2,1,0:T(2,128)(2,1)}, u32[]{:S(2)}, u32[]{:S(2)}) collective-permute-start(bf16[5,1,2048]{2,1,0:T(2,128)(2,1)} %get-tuple-element.916), channel_id=1, source_target_pairs={{0,1},{1,2},{2,3},{3,4},{4,5},{5,6},{6,7},{8,9},{9,10},{10,11},{11... | collective-permute-start | bytes 61448 | tf_op jit(solution)/shard_map/ppermute | solution.py:15
  545.6 37.1 %collective-permute-start.27 = (bf16[5,1,2048]{2,1,0:T(2,128)(2,1)}, bf16[5,1,2048]{2,1,0:T(2,128)(2,1)}, u32[]{:S(2)}, u32[]{:S(2)}) collective-permute-start(bf16[5,1,2048]{2,1,0:T(2,128)(2,1)} %get-tuple-element.917), channel_id=1, source_target_pairs={{1,0},{2,1},{3,2},{4,3},{5,4},{6,5},{7,6},{9,8},{10,9},{11,10},{12... | collective-permute-start | bytes 61448 | tf_op jit(solution)/shard_map/ppermute | solution.py:17
  585.5 35.8 %copy-start.3 = (bf16[5,10,66,32]{3,2,1,0:T(8,128)(2,1)S(1)}, bf16[5,10,66,32]{3,2,1,0:T(8,128)(2,1)}, u32[]{:S(2)}) copy-start(bf16[5,10,66,32]{3,2,1,0:T(8,128)(2,1)} %copy-done.2) | copy-start | bytes 633604
  659.6 4.5 collective-permute-start.28
  661.8 6.1 collective-permute-start.29
  668.0 4.9 collective-permute-start.30
  670.0 5.2 collective-permute-start.31
  708.7 239.0 %copy-start.1 = (bf16[1,32,104]{2,1,0:T(8,128)(2,1)S(1)}, bf16[1,32,104]{2,1,0:T(8,128)(2,1)}, u32[]{:S(2)}) copy-start(bf16[1,32,104]{2,1,0:T(8,128)(2,1)} %param.32) | copy-start | bytes 19972
  (16 other events, 86.8 us)
Sparse Core Ops, SparseCore 0:
  229.2 84.2 all-gather.1
  673.0 272.9 all-reduce.9
